TPU v7x, 32 devices: a whole 2x2x4 slice. The times are simulated.
32 devices in a mesh: tm: 8 (over z, x), space: 4 (over y, core).
Axes of the slice: x: 2, y: 2, z: 4, core: 2. Of those that a mesh axis runs over, the one named last changes fastest.
Arguments:
- tokens: bfloat16 [16384, 2240], P(('tm', 'space')), may hold values from -8 to 8, as said below
- tangents: bfloat16 [16384, 2240], P(('tm', 'space')), may hold values from -6 to 6
- w_query: bfloat16 [2240, 560], replicated, may hold values from -0.125 to 0.125
- w_key: bfloat16 [2240, 560], replicated, may hold values from -0.125 to 0.125
- w_value: bfloat16 [2240, 560], replicated, may hold values from -0.125 to 0.125
Outputs:
- attended: bfloat16 [16384, 560], P(('tm', 'space'))
- attended_tangent: bfloat16 [16384, 560], P(('tm', 'space'))
Inputs may be any that keep to these rules, and one draw needn't show every extreme that they name: `tokens`: activations of every token, each spread about an offset that varies by feature and by group of rows.
All inputs are finite; a program needn't handle non-finite values.
Results may differ from a plain program's by a relative error of at most 0.018.
Values sent between devices are 32-bit elements; how exact they have to be, the bound alone decides.
A program may use at most 64 MiB of HBM per device.

v0:
```python
import jax
import jax.numpy as jnp
from jax import lax
from jax.sharding import PartitionSpec as P

HD = 112
HEADS = 5


epsilon = 1e-06


def carried_in(part, axis, combine, identity):
    place = lax.axis_index(axis)
    gathered = jax.tree.map(lambda a: lax.all_gather(a, axis), part)
    state = jax.tree.map(lambda a, e: jnp.zeros_like(a) + jnp.asarray(e, a.dtype), part, identity)

    def one(step, state):
        return combine(
            state, jax.tree.map(lambda a: lax.dynamic_index_in_dim(a, step, 0, False), gathered)
        )

    return lax.fori_loop(0, place, one, state)


def project(source, w_query, w_key, w_value):
    return tuple(
        (
            jnp.dot(source, weight, preferred_element_type=jnp.float32)
            .astype(jnp.bfloat16)
            .reshape(source.shape[0], HEADS, HD)
            for weight in (w_query, w_key, w_value)
        )
    )


def add_states(earlier, later):
    return tuple((first_part + second_part for first_part, second_part in zip(earlier, later)))


def shards(tokens, tangents, w_query, w_key, w_value):
    highest = lax.Precision.HIGHEST
    queries, key_rows, values = project(tokens, w_query, w_key, w_value)
    query_tangent, key_tangent, value_tangent = project(tangents, w_query, w_key, w_value)
    key_feature = jnp.maximum(key_rows, jnp.zeros_like(key_rows))
    feature_tangent = jnp.where(key_rows > 0, key_tangent, jnp.zeros_like(key_tangent))
    state_main = jnp.einsum("lhd,lhe->hde", key_feature, values, preferred_element_type=jnp.float32)
    state_tangent = jnp.einsum(
        "lhd,lhe->hde", feature_tangent, values, preferred_element_type=jnp.float32
    ) + jnp.einsum("lhd,lhe->hde", key_feature, value_tangent, preferred_element_type=jnp.float32)
    norm_main = jnp.sum(key_feature.astype(jnp.float32), axis=0)
    norm_tangent = jnp.sum(feature_tangent.astype(jnp.float32), axis=0)
    local_states = (state_main, state_tangent, norm_main, norm_tangent)
    block_states = lax.psum(
        (local_states[0], local_states[1], local_states[2], local_states[3]), "space"
    )
    empty_states = tuple((jnp.zeros_like(element) for element in block_states))
    before = carried_in(block_states, "tm", add_states, empty_states)
    totals = add_states(before, block_states)
    seen, seen_tangent, seen_norm, seen_norm_tangent = totals
    query_feature = jnp.maximum(queries, jnp.zeros_like(queries)).astype(jnp.float32)
    query_slope = jnp.where(queries > 0, query_tangent, jnp.zeros_like(query_tangent)).astype(
        jnp.float32
    )
    numer = jnp.einsum("lhd,hde->lhe", query_feature, seen, precision=highest)
    denom = jnp.einsum("lhd,hd->lh", query_feature, seen_norm, precision=highest) + epsilon
    numer_tangent = jnp.einsum("lhd,hde->lhe", query_slope, seen, precision=highest) + jnp.einsum(
        "lhd,hde->lhe", query_feature, seen_tangent, precision=highest
    )
    denom_tangent = jnp.einsum(
        "lhd,hd->lh", query_slope, seen_norm, precision=highest
    ) + jnp.einsum("lhd,hd->lh", query_feature, seen_norm_tangent, precision=highest)
    denom = denom[..., None]
    denom_tangent = denom_tangent[..., None]
    row_total = queries.shape[0]
    attended = (numer / denom).astype(jnp.bfloat16).reshape(row_total, HEADS * HD)
    attended_tangent = (
        (numer_tangent / denom - numer * denom_tangent / (denom * denom))
        .astype(jnp.bfloat16)
        .reshape(row_total, HEADS * HD)
    )
    return (attended, attended_tangent)


def solution(mesh):
    in_specs = (P(("tm", "space"), None), P(("tm", "space"), None), P(), P(), P())
    out_specs = (P(("tm", "space"), None), P(("tm", "space"), None))
    return jax.shard_map(shards, mesh=mesh, in_specs=in_specs, out_specs=out_specs, check_vma=False)
```

profile of v0, /device:TPU:27, one launch (start us, length us, event | category | flops | bytes accessed | tf_op | source)
XLA Modules:
  0.0 181.5 jit_solution(16407765304645862956)
XLA Ops:
  7.2 1.7 copy-done
  8.9 3.3 %broadcast_maximum_fusion.1 = (bf16[512,560]{0,1:T(8,128)(2,1)S(1)}, bf16[512,560]{0,1:T(8,128)(2,1)S(1)}) fusion(bf16[2240,560]{0,1:T(8,128)(2,1)S(1)} %copy-done, bf16[512,2240]{0,1:T(8,128)(2,1)} %param.7), kind=kOutput, calls=%fused_computation.24 | convolution fusion | flops 1285079040 | bytes 5949440 | tf_op jit(solution)/shard_map/dot_general | solution.py:29
  12.2 1.5 convolution_convert_fusion.4
  13.9 1.5 convolution_convert_fusion.2
  15.4 1.6 convert_reduce_fusion
  19.4 33.9 %all-reduce.4.cloned.1.call-done = (f32[5,112,112]{2,1,0:T(8,128)}, f32[5,112,112]{2,1,0:T(8,128)}) async-done(((f32[5,112,112]{2,1,0:T(8,128)}, f32[5,112,112]{2,1,0:T(8,128)}), (f32[5,112,112]{2,1,0:T(8,128)}, f32[5,112,112]{2,1,0:T(8,128)})) %all-reduce.4.cloned.1.call-update) | async-done | bytes 501776 | tf_op jit(solution)/shard_map/psum | solution.py:54
  54.5 6.5 %all-reduce = (f32[5,112]{1,0:T(8,128)S(1)}, f32[5,112]{1,0:T(8,128)S(1)}) all-reduce(f32[5,112]{1,0:T(8,128)S(1)} %reduce_sum.23, f32[5,112]{1,0:T(8,128)S(1)} %reduce_sum.25), channel_id=1, replica_groups=mesh['tm'=8,'space'=4] {'space'}, use_global_device_ids=true, to_apply=%region_3.4 | all-reduce | flops 1120 | bytes 8960 | tf_op jit(solution)/shard_map/psum | solution.py:54
  60.9 24.4 %all-gather.4 = f32[8,5,112]{2,1,0:T(8,128)S(1)} all-gather(f32[1,5,112]{2,1,0:T(8,128)S(1)} %bitcast.94), channel_id=4, replica_groups=mesh['tm'=8,'space'=4] {'tm'}, dimensions={0}, use_global_device_ids=true | all-gather | bytes 20160 | tf_op jit(solution)/shard_map/all_gather | solution.py:15
  85.3 25.0 %all-gather.5 = f32[8,5,112]{2,1,0:T(8,128)S(1)} all-gather(f32[1,5,112]{2,1,0:T(8,128)S(1)} %bitcast.95), channel_id=5, replica_groups=mesh['tm'=8,'space'=4] {'tm'}, dimensions={0}, use_global_device_ids=true | all-gather | bytes 20160 | tf_op jit(solution)/shard_map/all_gather | solution.py:15
  110.3 4.9 %broadcast_maximum_fusion = (bf16[512,560]{0,1:T(8,128)(2,1)}, bf16[512,560]{0,1:T(8,128)(2,1)S(1)}) fusion(bf16[2240,560]{0,1:T(8,128)(2,1)} %param.9, bf16[512,2240]{0,1:T(8,128)(2,1)} %param.7), kind=kOutput, calls=%fused_computation.23 | convolution fusion | flops 1285079040 | bytes 5949440 | tf_op jit(solution)/shard_map/dot_general | solution.py:29
  115.2 2.3 %fusion.5 = bf16[512,560]{0,1:T(8,128)(2,1)} fusion(bf16[2240,560]{0,1:T(8,128)(2,1)S(1)} %copy-done.5, bf16[512,2240]{0,1:T(8,128)(2,1)S(1)} %copy-done.8, bf16[512,560]{0,1:T(8,128)(2,1)S(1)} %get-tuple-element.91), kind=kOutput, calls=%fused_computation.17 | convolution fusion | flops 1285365760 | bytes 5949440 | tf_op jit(solution)/shard_map/dot_general | solution.py:29
  117.5 39.3 %all-gather.11.cloned.1.call-done = f32[40,112,112]{2,1,0:T(8,128)} async-done(((f32[5,112,112]{2,1,0:T(8,128)}), f32[40,112,112]{2,1,0:T(8,128)}) %all-gather.11.cloned.1.call-update) | async-done | bytes 2007056 | tf_op jit(solution)/shard_map/all_gather | solution.py:15
  156.9 8.8 %while.16 = (s32[]{:T(128)}, f32[5,112,112]{2,1,0:T(8,128)S(1)}, f32[5,112,112]{2,1,0:T(8,128)S(1)}, f32[5,112]{1,0:T(8,128)S(1)}, f32[5,112]{1,0:T(8,128)S(1)},...) while((s32[]{:T(128)}, f32[5,112,112]{2,1,0:T(8,128)S(1)}, ...), condition=%wide.region_7.8_spmd, body=%wide.region_6.7_spmd.sunk | while | flops 126565 | bytes 1518887 | solution.py:23
  156.9 1.2 bitcast_add_fusion.8
  158.2 1.2 bitcast_add_fusion.8
  159.5 1.2 bitcast_add_fusion.8
  160.7 1.2 bitcast_add_fusion.8
  162.0 1.2 bitcast_add_fusion.8
  165.7 1.4 fusion.17
  167.2 1.4 fusion.15
  168.6 1.4 fusion.12
  170.0 1.7 fusion.7
  171.7 1.5 divide_convert_fusion
  173.3 1.7 fusion.3
  (47 shorter events, 6.3 us)
Async XLA Ops:
  7.2 1.7 copy-start
  7.2 46.2 %all-reduce.4.cloned.1.call-start = ((), (), s32[]{:S(2)}) async-start(), calls=%async_computation.2 | async-start | bytes 1146880 | tf_op jit(solution)/shard_map/psum | solution.py:54
  8.9 3.3 %copy-start.4 = (bf16[2240,560]{0,1:T(8,128)(2,1)S(1)}, bf16[2240,560]{0,1:T(8,128)(2,1)}, u32[]{:S(2)}) copy-start(bf16[2240,560]{0,1:T(8,128)(2,1)} %param.11) | copy-start | bytes 7526404
  8.9 3.3 %copy-start.6 = (bf16[512,2240]{0,1:T(8,128)(2,1)S(1)}, bf16[512,2240]{0,1:T(8,128)(2,1)}, u32[]{:S(2)}) copy-start(bf16[512,2240]{0,1:T(8,128)(2,1)} %param.7) | copy-start | bytes 6881284
  12.2 1.6 copy-start.7
  19.4 98.2 %all-gather.9.cloned.1.call-start = ((), (), s32[]{:S(2)}) async-start(), calls=%async_computation | async-start | bytes 2580480 | tf_op jit(solution)/shard_map/all_gather | solution.py:15
  53.4 103.5 %all-gather.11.cloned.1.call-start = ((), (), s32[]{:S(2)}) async-start(), calls=%async_computation.1 | async-start | bytes 2580480 | tf_op jit(solution)/shard_map/all_gather | solution.py:15
  110.3 4.9 %copy-start.5 = (bf16[2240,560]{0,1:T(8,128)(2,1)S(1)}, bf16[2240,560]{0,1:T(8,128)(2,1)}, u32[]{:S(2)}) copy-start(bf16[2240,560]{0,1:T(8,128)(2,1)} %param.9) | copy-start | bytes 7526404
  110.3 4.9 %copy-start.8 = (bf16[512,2240]{0,1:T(8,128)(2,1)S(1)}, bf16[512,2240]{0,1:T(8,128)(2,1)}, u32[]{:S(2)}) copy-start(bf16[512,2240]{0,1:T(8,128)(2,1)} %param.8) | copy-start | bytes 6881284
  156.9 13.1 %copy-start.2 = (f32[5,112,112]{2,1,0:T(8,128)S(1)}, f32[5,112,112]{2,1,0:T(8,128)}, u32[]{:S(2)}) copy-start(f32[5,112,112]{2,1,0:T(8,128)} %get-tuple-element.84) | copy-start | bytes 752644
  165.7 6.0 %copy-start.1 = (bf16[512,560]{0,1:T(8,128)(2,1)S(1)}, bf16[512,560]{0,1:T(8,128)(2,1)}, u32[]{:S(2)}) copy-start(bf16[512,560]{0,1:T(8,128)(2,1)} %get-tuple-element.90) | copy-start | bytes 1720324
  171.7 1.5 copy-start.3
Sparse Core Ops, SparseCore 0:
  19.5 33.8 all-reduce.3
  55.5 49.4 all-gather.8
  107.2 49.6 all-gather.10
where the time goes:
time: 183 us; the launch traced here: 181 us
  waiting for transfers between devices  73.9 us (40%)
  blocking collectives  55.9 us (31%)
  matrix products  26.5 us (14%)
  between operations  13.9 us (8%)
  other arithmetic  8.76 us (5%)
  local copies, waits for them, and re-layouts  2.05 us (1%)
    all_gather x2, blocking collectives, carried_in(): gathered = jax.tree.map(lambda a: lax.all_gather(a, axis), part)  49.4 us
    all_gather x2, waiting for transfers between devices, carried_in(): gathered = jax.tree.map(lambda a: lax.all_gather(a, axis), part)  39.3 us
    psum x1, waiting for transfers between devices, shards(): lax.psum((local_states[0], local_states[1], local_states[2], local_states...  33.9 us
    dot_general x6, matrix products, project(): jnp.dot(source, weight, preferred_element_type=jnp.float32)  15.1 us
    add x15, other arithmetic, add_states(): first_part + second_part  8.55 us
    psum x1, blocking collectives, shards(): lax.psum((local_states[0], local_states[1], local_states[2], local_states...  6.48 us
  transfers between devices with their start and end apart: 3, of which 2 were waited for; matrix products, arithmetic and copies ran while one was open for 4% of the time, Pallas kernels for 0%

commit v1 on v0

v1 whole, which is shorter than its diff:
```python
import functools

import jax
import jax.numpy as jnp
from jax import lax
from jax.experimental import pallas as pl
from jax.experimental.pallas import tpu as pltpu
from jax.sharding import PartitionSpec as P

HD = 112
HEADS = 5
WIDE = 128
EPSILON = 1e-06
MESH = pl.DeviceIdType.MESH


def dot(a, b, dims=((1,), (0,))):
    return lax.dot_general(a, b, (dims, ((), ())), preferred_element_type=jnp.float32)


def kernel(
    n_tm, n_space, rows,
    tok_hbm, tan_hbm, wq_hbm, wk_hbm, wv_hbm,
    att_ref, att_t_ref,
    tok, tan, wq, wk, wv, load_sem,
    kbuf, vbuf, ktbuf, vtbuf, qbuf, qtbuf,
    state, r1, abuf, r2, bbuf, r3, erecv, esend, xsend, full,
    s1, q1, s2, q2, s3, q3, s4, q4, s5, q5, s6, q6, s7, q7,
):
    ny, nz = n_space // 2, n_tm // 2
    half, quarter, eighth = rows // 2, rows // n_space, rows // (2 * n_space)
    tm, space = lax.axis_index("tm"), lax.axis_index("space")
    core, y = lax.rem(space, 2), space // 2
    x, z = lax.rem(tm, 2), tm // 2
    core_mate = space + 1 - 2 * core
    x_mate = tm + 1 - 2 * x
    z_next, z_prev = lax.rem(tm + 2, n_tm), lax.rem(tm + n_tm - 2, n_tm)

    def y_mate(k):
        return 2 * lax.rem(y + k, ny) + core

    def load(i, src, dst):
        return pltpu.make_async_copy(src, dst, load_sem.at[i])

    loads = [
        load(0, tok_hbm, tok), load(1, wk_hbm, wk), load(2, wv_hbm, wv),
        load(3, tan_hbm, tan), load(4, wq_hbm, wq),
    ]
    for one in loads:
        one.start()

    barrier = pltpu.get_barrier_semaphore()
    partners = [{"space": core_mate}, {"tm": x_mate}, {"tm": z_next}, {"tm": z_prev}]
    partners += [{"space": y_mate(k)} for k in range(1, ny)]
    for partner in partners:
        pl.semaphore_signal(barrier, inc=1, device_id=partner, device_id_type=MESH)

    def rows_at(start, count):
        return pl.ds(pl.multiple_of(start, 8), count)

    half_mine = core * half
    quarter_mine = half_mine + y * quarter

    def send(src, dst, ssem, rsem, device):
        return pltpu.make_async_remote_copy(
            src_ref=src, dst_ref=dst, send_sem=ssem, recv_sem=rsem,
            device_id=device, device_id_type=MESH,
        )

    def copy1(g):
        return send(
            state.at[g, rows_at((1 - core) * half, half)], r1.at[g],
            s1.at[g], q1.at[g], {"space": core_mate},
        )

    def copy2(g, k):
        return send(
            abuf.at[g, rows_at(lax.rem(y + k, ny) * quarter, quarter)], r2.at[g, k - 1],
            s2.at[g, k - 1], q2.at[g, k - 1], {"space": y_mate(k)},
        )

    def copy3(g):
        return send(
            bbuf.at[g, rows_at((1 - x) * eighth, eighth)], r3.at[g],
            s3.at[g], q3.at[g], {"tm": x_mate},
        )

    def copy4(g):
        return send(esend.at[g], erecv.at[g], s4.at[g], q4.at[g], {"tm": z_next})

    def copy5(g):
        return send(
            xsend.at[g], full.at[g, rows_at(quarter_mine + x * eighth, eighth)],
            s5.at[g], q5.at[g], {"tm": x_mate},
        )

    def copy6(g, k):
        part = full.at[g, rows_at(quarter_mine, quarter)]
        return send(part, part, s6.at[g, k - 1], q6.at[g, k - 1], {"space": y_mate(k)})

    def copy7(g, k):
        part = full.at[g, rows_at(half_mine + lax.rem(y + ny - k, ny) * quarter, quarter)]
        return send(part, part, s7.at[g, k], q7.at[g, k], {"space": core_mate})

    def stage1(g):
        copy1(g).start()

    def stage2(g):
        copy1(g).wait_recv()
        abuf[g] = state[g, rows_at(half_mine, half)] + r1[g]
        for k in range(1, ny):
            copy2(g, k).start()

    def stage3(g):
        total = abuf[g, rows_at(y * quarter, quarter)]
        for k in range(1, ny):
            copy2(g, k).wait_recv()
            total = total + r2[g, k - 1]
        bbuf[g] = total
        copy3(g).start()

    def stage4(g):
        copy3(g).wait_recv()
        own = bbuf[g, rows_at(x * eighth, eighth)]

        @pl.when(z == 0)
        def _():
            erecv[g] = jnp.zeros((eighth, WIDE), jnp.float32)

        @pl.when(z > 0)
        def _():
            copy4(g).wait_recv()

        before, other = erecv[g], r3[g]
        first = before + other
        pair = first + own

        @pl.when(z < nz - 1)
        def _():
            esend[g] = pair
            copy4(g).start()

        mine_first = x == 0
        xsend[g] = jnp.where(mine_first, pair, first)
        copy5(g).start()
        full[g, rows_at(quarter_mine + x * eighth, eighth)] = jnp.where(
            mine_first, before + own, pair
        )

    def stage6(g):
        copy5(g).wait_recv()
        for k in range(1, ny):
            copy6(g, k).start()
        copy7(g, 0).start()

    def stage7(g):
        for k in range(1, ny):
            copy6(g, k).wait_recv()
            copy7(g, k).start()

    def finish(g):
        for k in range(ny):
            copy7(g, k).wait_recv()

    def drain(g):
        copy1(g).wait_send()
        for k in range(1, ny):
            copy2(g, k).wait_send()
            copy6(g, k).wait_send()
        copy3(g).wait_send()

        @pl.when(z < nz - 1)
        def _():
            copy4(g).wait_send()

        copy5(g).wait_send()
        for k in range(ny):
            copy7(g, k).wait_send()

    def project(source, weight, out):
        out[...] = dot(source[...], weight[...]).astype(jnp.bfloat16)

    count = tok.shape[0]

    def head(ref, h):
        return ref[:, h * HD : (h + 1) * HD]

    def values_of(ref, h, fill):
        tail = jnp.where(
            lax.broadcasted_iota(jnp.int32, (count, WIDE - HD), 1) == 0, fill, 0.0
        ).astype(jnp.bfloat16)
        return jnp.concatenate([head(ref, h), tail], axis=1)

    for g in range(2):
        state[g, rows_at(HEADS * HD, rows - HEADS * HD)] = jnp.zeros(
            (rows - HEADS * HD, WIDE), jnp.float32
        )
    loads[0].wait()
    loads[1].wait()
    project(tok, wk, kbuf)
    loads[2].wait()
    project(tok, wv, vbuf)
    over = ((0,), (0,))
    zero = jnp.zeros((), jnp.bfloat16)
    for h in range(HEADS):
        feature = jnp.maximum(head(kbuf, h), zero)
        state[0, h * HD : (h + 1) * HD] = dot(feature, values_of(vbuf, h, 1.0), over)
    pl.semaphore_wait(barrier, len(partners))
    stage1(0)
    loads[3].wait()
    project(tan, wk, ktbuf)
    stage2(0)
    project(tan, wv, vtbuf)
    for h in range(HEADS):
        keys = head(kbuf, h)
        feature = jnp.maximum(keys, zero)
        slope = jnp.where(keys > 0, head(ktbuf, h), zero)
        state[1, h * HD : (h + 1) * HD] = dot(slope, values_of(vbuf, h, 1.0), over) + dot(
            feature, values_of(vtbuf, h, 0.0), over
        )
    stage1(1)
    stage3(0)
    loads[4].wait()
    project(tok, wq, qbuf)
    stage2(1)
    stage4(0)
    project(tan, wq, qtbuf)
    stage3(1)
    stage4(1)
    stage6(0)
    stage7(0)
    stage6(1)
    finish(0)
    stage7(1)
    finish(1)

    pad_rows = jnp.zeros((WIDE - HD, WIDE), jnp.float32)
    pad_lanes = jnp.zeros((count, WIDE - HD), jnp.bfloat16)
    empty = jnp.zeros((WIDE, WIDE), jnp.float32)
    for h in range(HEADS):
        queries = head(qbuf, h)
        feature = jnp.maximum(queries, zero)
        slope = jnp.where(queries > 0, head(qtbuf, h), zero)
        left = jnp.concatenate([feature, pad_lanes, slope, pad_lanes], axis=1)
        seen = jnp.concatenate([full[0, h * HD : (h + 1) * HD], pad_rows], axis=0)
        seen_t = jnp.concatenate([full[1, h * HD : (h + 1) * HD], pad_rows], axis=0)
        right = jnp.concatenate(
            [
                jnp.concatenate([seen, seen_t], axis=1),
                jnp.concatenate([empty, seen], axis=1),
            ],
            axis=0,
        )
        high = right.astype(jnp.bfloat16)
        low = (right - high.astype(jnp.float32)).astype(jnp.bfloat16)
        both = dot(left, high) + dot(left, low)
        main, slant = both[:, :WIDE], both[:, WIDE:]
        inverse = 1.0 / (main[:, HD : HD + 1] + EPSILON)
        denom_t = slant[:, HD : HD + 1]
        attended = main * inverse
        tangent = (slant - attended * denom_t) * inverse
        att_ref[:, h * HD : (h + 1) * HD] = attended[:, :HD].astype(att_ref.dtype)
        att_t_ref[:, h * HD : (h + 1) * HD] = tangent[:, :HD].astype(att_t_ref.dtype)
    for g in range(2):
        drain(g)


def solution(mesh):
    n_tm, n_space = mesh.shape["tm"], mesh.shape["space"]
    ny = n_space // 2
    unit = 8 * 2 * n_space
    rows = (HEADS * HD + unit) // unit * unit

    def step(tokens, tangents, w_query, w_key, w_value):
        count, width = tokens.shape
        out = w_query.shape[1]
        bf16, f32 = jnp.bfloat16, jnp.float32
        quarter, eighth = rows // n_space, rows // (2 * n_space)
        dma = pltpu.SemaphoreType.DMA
        sems = []
        for shape in ((2,), (2, ny - 1), (2,), (2,), (2,), (2, ny - 1), (2, ny)):
            sems += [dma(shape), dma(shape)]
        return tuple(pl.pallas_call(
            functools.partial(kernel, n_tm, n_space, rows),
            out_shape=[jax.ShapeDtypeStruct((count, out), bf16)] * 2,
            in_specs=[pl.BlockSpec(memory_space=pl.ANY)] * 5,
            out_specs=[pl.BlockSpec(memory_space=pltpu.VMEM)] * 2,
            scratch_shapes=[
                pltpu.VMEM((count, width), bf16),
                pltpu.VMEM((count, width), bf16),
                pltpu.VMEM((width, out), bf16),
                pltpu.VMEM((width, out), bf16),
                pltpu.VMEM((width, out), bf16),
                dma((5,)),
            ]
            + [pltpu.VMEM((count, out), bf16)] * 6
            + [
                pltpu.VMEM((2, rows, WIDE), f32),
                pltpu.VMEM((2, rows // 2, WIDE), f32),
                pltpu.VMEM((2, rows // 2, WIDE), f32),
                pltpu.VMEM((2, ny - 1, quarter, WIDE), f32),
                pltpu.VMEM((2, quarter, WIDE), f32),
                pltpu.VMEM((2, eighth, WIDE), f32),
                pltpu.VMEM((2, eighth, WIDE), f32),
                pltpu.VMEM((2, eighth, WIDE), f32),
                pltpu.VMEM((2, eighth, WIDE), f32),
                pltpu.VMEM((2, rows, WIDE), f32),
            ]
            + sems,
            compiler_params=pltpu.CompilerParams(
                collective_id=0, has_side_effects=True, vmem_limit_bytes=60 * 1024 * 1024
            ),
        )(tokens, tangents, w_query, w_key, w_value))

    both = P(("tm", "space"), None)
    return jax.shard_map(
        step, mesh=mesh, in_specs=(both, both, P(), P(), P()), out_specs=(both, both),
        check_vma=False,
    )
```

time: 183 us -> 67.8 us (0.37)
  waiting for transfers between devices: 73.9 us -> 0 us
  blocking collectives: 55.9 us -> 0 us
  Pallas kernels: 0 us -> 42.9 us
  matrix products: 26.5 us -> 0 us
  local copies, waits for them, and re-layouts: 2.05 us -> 23.4 us
  between operations: 13.9 us -> 0.64 us
  other arithmetic: 8.76 us -> 0 us
    all_gather x2 -> x0, blocking collectives: 49.4 us -> none  [carried_in(): gathered = jax.tree.map(lambda a: lax.all_gather(a, axis), part)]
    pallas_call x0 -> x1, Pallas kernels: none -> 42.9 us  [step(): pl.pallas_call(functools.partial(kernel, n_tm, n_space, rows), out_shape=...]
    all_gather x2 -> x0, waiting for transfers between devices: 39.3 us -> none  [carried_in(): gathered = jax.tree.map(lambda a: lax.all_gather(a, axis), part)]
    psum x1 -> x0, waiting for transfers between devices: 33.9 us -> none  [shards(): lax.psum((local_states[0], local_states[1], local_states[2], local_states...]
    dot_general x15 -> x0, matrix products: 26.5 us -> none  [the longest x6 15.1 us: project(): jnp.dot(source, weight, preferred_element_type=jnp.float32)]
    unnamed x18 -> x9, local copies, waits for them, and re-layouts: 1.85 us -> 19.1 us
    add x17 -> x0, other arithmetic: 8.56 us -> none  [the longest x15 8.55 us: add_states(): first_part + second_part]
    psum x1 -> x0, blocking collectives: 6.48 us -> none  [shards(): lax.psum((local_states[0], local_states[1], local_states[2], local_states...]
  transfers between devices with their start and end apart: 3 -> 0, of which waited for: 2 -> 0; matrix products, arithmetic and copies ran while one was open for 4% -> 0% of each run, Pallas kernels for 0% -> 0%
where the time goes in v1:
time: 67.8 us; the launch traced here: 66.9 us
  Pallas kernels  42.9 us (63%)
  local copies, waits for them, and re-layouts  23.4 us (35%)
    pallas_call x1, Pallas kernels, step(): pl.pallas_call(functools.partial(kernel, n_tm, n_space, rows), out_shape=...  42.9 us
    unnamed x9, local copies, waits for them, and re-layouts  19.1 us
    pallas_call x2, local copies, waits for them, and re-layouts, step(): pl.pallas_call(functools.partial(kernel, n_tm, n_space, rows), out_shape=...  4.24 us

profile of v1, /device:TPU:27, one launch (start us, length us, event | category | flops | bytes accessed | tf_op | source)
XLA Modules:
  0.0 66.9 jit_solution(17865535089154473185)
XLA Ops:
  0.6 4.3 %copy.7.tok_hbm = bf16[512,2240]{1,0:T(8,128)(2,1)} copy(bf16[512,2240]{0,1:T(8,128)(2,1)} %param.5) | data formatting | bytes 4587520 | tf_op args[0]
  4.9 0.0 copy-start
  4.9 4.4 %copy.8.tan_hbm = bf16[512,2240]{1,0:T(8,128)(2,1)} copy(bf16[512,2240]{0,1:T(8,128)(2,1)} %param.6) | data formatting | bytes 4587520 | tf_op args[1]
  9.3 0.0 copy-done
  9.3 2.9 %copy.9.wq_hbm = bf16[2240,560]{1,0:T(8,128)(2,1)} copy(bf16[2240,560]{0,1:T(8,128)(2,1)S(1)} %copy-done) | data formatting | bytes 5017600 | tf_op args[2]
  12.2 0.0 copy-start.1
  12.2 4.6 %copy.10.wk_hbm = bf16[2240,560]{1,0:T(8,128)(2,1)} copy(bf16[2240,560]{0,1:T(8,128)(2,1)} %param.8) | data formatting | bytes 5017600 | tf_op args[3]
  16.8 0.0 copy-done.1
  16.8 3.0 %copy.11.wv_hbm = bf16[2240,560]{1,0:T(8,128)(2,1)} copy(bf16[2240,560]{0,1:T(8,128)(2,1)S(1)} %copy-done.1) | data formatting | bytes 5017600 | tf_op args[4]
  19.8 42.9 %shard_map.68 = (bf16[512,560]{1,0:T(8,128)(2,1)}, bf16[512,560]{1,0:T(8,128)(2,1)}) custom-call(bf16[512,2240]{1,0:T(8,128)(2,1)} %copy.7.tok_hbm, bf16[512,2240]{1,0:T(8,128)(2,1)} %copy.8.tan_hbm, bf16[2240,560]{1,0:T(8,128)(2,1)} %copy.9.wq_hbm, bf16[2240,560]{1,0:T(8,128)(2,1)} %copy.10.wk_hbm, bf16[2240,560]{1,0:T(8,128)(2,1)} %copy.11.wv_hbm), custom_call_target="tpu_custom_call" | custom-call | tf_op jit(solution)/shard_map/pallas_call | solution.py:283
  62.7 2.1 %copy.12 = bf16[512,560]{0,1:T(8,128)(2,1)} copy(bf16[512,560]{1,0:T(8,128)(2,1)} %get-tuple-element.2) | data formatting | bytes 1146880 | tf_op jit(solution)/shard_map/pallas_call | solution.py:283
  64.8 2.1 %copy.13 = bf16[512,560]{0,1:T(8,128)(2,1)} copy(bf16[512,560]{1,0:T(8,128)(2,1)} %get-tuple-element.3) | data formatting | bytes 1146880 | tf_op jit(solution)/shard_map/pallas_call | solution.py:283
Async XLA Ops:
  4.9 4.4 %copy-start = (bf16[2240,560]{0,1:T(8,128)(2,1)S(1)}, bf16[2240,560]{0,1:T(8,128)(2,1)}, u32[]{:S(2)}) copy-start(bf16[2240,560]{0,1:T(8,128)(2,1)} %param.7) | copy-start | bytes 7526404
  12.2 4.6 %copy-start.1 = (bf16[2240,560]{0,1:T(8,128)(2,1)S(1)}, bf16[2240,560]{0,1:T(8,128)(2,1)}, u32[]{:S(2)}) copy-start(bf16[2240,560]{0,1:T(8,128)(2,1)} %param.9) | copy-start | bytes 7526404

commit v2 on v1

--- a/solution.py
+++ b/solution.py
@@ -178,18 +178,18 @@
             copy7(g, k).wait_send()
 
     def project(source, weight, out):
-        out[...] = dot(source[...], weight[...]).astype(jnp.bfloat16)
-
-    count = tok.shape[0]
+        out[...] = dot(weight[...], source[...]).astype(jnp.bfloat16)
+
+    count = tok.shape[1]
 
     def head(ref, h):
-        return ref[:, h * HD : (h + 1) * HD]
+        return ref[h * HD : (h + 1) * HD]
+
+    first_row = lax.broadcasted_iota(jnp.int32, (WIDE - HD, count), 0) == 0
 
     def values_of(ref, h, fill):
-        tail = jnp.where(
-            lax.broadcasted_iota(jnp.int32, (count, WIDE - HD), 1) == 0, fill, 0.0
-        ).astype(jnp.bfloat16)
-        return jnp.concatenate([head(ref, h), tail], axis=1)
+        tail = jnp.where(first_row, fill, 0.0).astype(jnp.bfloat16)
+        return jnp.concatenate([head(ref, h), tail], axis=0)
 
     for g in range(2):
         state[g, rows_at(HEADS * HD, rows - HEADS * HD)] = jnp.zeros(
@@ -200,7 +200,7 @@
     project(tok, wk, kbuf)
     loads[2].wait()
     project(tok, wv, vbuf)
-    over = ((0,), (0,))
+    over = ((1,), (1,))
     zero = jnp.zeros((), jnp.bfloat16)
     for h in range(HEADS):
         feature = jnp.maximum(head(kbuf, h), zero)
@@ -234,33 +234,31 @@
     stage7(1)
     finish(1)
 
-    pad_rows = jnp.zeros((WIDE - HD, WIDE), jnp.float32)
-    pad_lanes = jnp.zeros((count, WIDE - HD), jnp.bfloat16)
-    empty = jnp.zeros((WIDE, WIDE), jnp.float32)
+    empty = jnp.zeros((HD, WIDE), jnp.float32)
     for h in range(HEADS):
         queries = head(qbuf, h)
         feature = jnp.maximum(queries, zero)
         slope = jnp.where(queries > 0, head(qtbuf, h), zero)
-        left = jnp.concatenate([feature, pad_lanes, slope, pad_lanes], axis=1)
-        seen = jnp.concatenate([full[0, h * HD : (h + 1) * HD], pad_rows], axis=0)
-        seen_t = jnp.concatenate([full[1, h * HD : (h + 1) * HD], pad_rows], axis=0)
-        right = jnp.concatenate(
+        sides = jnp.concatenate([feature, slope], axis=0)
+        seen, seen_t = head(full.at[0], h), head(full.at[1], h)
+        maps = jnp.concatenate(
             [
                 jnp.concatenate([seen, seen_t], axis=1),
                 jnp.concatenate([empty, seen], axis=1),
             ],
             axis=0,
         )
-        high = right.astype(jnp.bfloat16)
-        low = (right - high.astype(jnp.float32)).astype(jnp.bfloat16)
-        both = dot(left, high) + dot(left, low)
-        main, slant = both[:, :WIDE], both[:, WIDE:]
-        inverse = 1.0 / (main[:, HD : HD + 1] + EPSILON)
-        denom_t = slant[:, HD : HD + 1]
-        attended = main * inverse
-        tangent = (slant - attended * denom_t) * inverse
-        att_ref[:, h * HD : (h + 1) * HD] = attended[:, :HD].astype(att_ref.dtype)
-        att_t_ref[:, h * HD : (h + 1) * HD] = tangent[:, :HD].astype(att_t_ref.dtype)
+        high = maps.astype(jnp.bfloat16)
+        low = (maps - high.astype(jnp.float32)).astype(jnp.bfloat16)
+        across = ((0,), (0,))
+        both = dot(high, sides, across) + dot(low, sides, across)
+        main, slant = both[:WIDE], both[WIDE:]
+        inverse = 1.0 / (main[HD : HD + 1] + EPSILON)
+        denom_t = slant[HD : HD + 1]
+        attended = main[:HD] * inverse
+        tangent = (slant[:HD] - attended * denom_t) * inverse
+        att_ref[h * HD : (h + 1) * HD] = attended.astype(att_ref.dtype)
+        att_t_ref[h * HD : (h + 1) * HD] = tangent.astype(att_t_ref.dtype)
     for g in range(2):
         drain(g)
 
@@ -280,20 +278,20 @@
         sems = []
         for shape in ((2,), (2, ny - 1), (2,), (2,), (2,), (2, ny - 1), (2, ny)):
             sems += [dma(shape), dma(shape)]
-        return tuple(pl.pallas_call(
+        outs = pl.pallas_call(
             functools.partial(kernel, n_tm, n_space, rows),
-            out_shape=[jax.ShapeDtypeStruct((count, out), bf16)] * 2,
+            out_shape=[jax.ShapeDtypeStruct((out, count), bf16)] * 2,
             in_specs=[pl.BlockSpec(memory_space=pl.ANY)] * 5,
             out_specs=[pl.BlockSpec(memory_space=pltpu.VMEM)] * 2,
             scratch_shapes=[
-                pltpu.VMEM((count, width), bf16),
-                pltpu.VMEM((count, width), bf16),
-                pltpu.VMEM((width, out), bf16),
-                pltpu.VMEM((width, out), bf16),
-                pltpu.VMEM((width, out), bf16),
+                pltpu.VMEM((width, count), bf16),
+                pltpu.VMEM((width, count), bf16),
+                pltpu.VMEM((out, width), bf16),
+                pltpu.VMEM((out, width), bf16),
+                pltpu.VMEM((out, width), bf16),
                 dma((5,)),
             ]
-            + [pltpu.VMEM((count, out), bf16)] * 6
+            + [pltpu.VMEM((out, count), bf16)] * 6
             + [
                 pltpu.VMEM((2, rows, WIDE), f32),
                 pltpu.VMEM((2, rows // 2, WIDE), f32),
@@ -310,7 +308,8 @@
             compiler_params=pltpu.CompilerParams(
                 collective_id=0, has_side_effects=True, vmem_limit_bytes=60 * 1024 * 1024
             ),
-        )(tokens, tangents, w_query, w_key, w_value))
+        )(tokens.T, tangents.T, w_query.T, w_key.T, w_value.T)
+        return outs[0].T, outs[1].T
 
     both = P(("tm", "space"), None)
     return jax.shard_map(

time: 67.8 us -> 41.2 us (0.61); the launches traced: 66.9 us -> 41 us
  local copies, waits for them, and re-layouts: 23.4 us -> 3.81 us
  Pallas kernels: 42.9 us -> 36.6 us
    unnamed x9 -> x2, local copies, waits for them, and re-layouts: 19.1 us -> 3.81 us
    pallas_call x1, Pallas kernels: 42.9 us -> 36.6 us  [step(): pl.pallas_call(functools.partial(kernel, n_tm, n_space, rows), out_shape=...]
    pallas_call x2 -> x0, local copies, waits for them, and re-layouts: 4.24 us -> none  [step(): pl.pallas_call(functools.partial(kernel, n_tm, n_space, rows), out_shape=...]
where the time goes in v2:
time: 41.2 us; the launch traced here: 41 us
  Pallas kernels  36.6 us (89%)
  local copies, waits for them, and re-layouts  3.81 us (9%)
  between operations  0.64 us (2%)
    pallas_call x1, Pallas kernels, step(): pl.pallas_call(functools.partial(kernel, n_tm, n_space, rows), out_shape=...  36.6 us
    unnamed x2, local copies, waits for them, and re-layouts  3.81 us

profile of v2, /device:TPU:27, one launch (start us, length us, event | category | flops | bytes accessed | tf_op | source)
XLA Modules:
  0.0 41.0 jit_solution(9824020567429050304)
XLA Ops:
  0.6 36.6 %shard_map.68 = (bf16[560,512]{1,0:T(8,128)(2,1)}, bf16[560,512]{1,0:T(8,128)(2,1)}) custom-call(bf16[2240,512]{1,0:T(8,128)(2,1)} %bitcast.10, bf16[2240,512]{1,0:T(8,128)(2,1)} %bitcast.11, bf16[560,2240]{1,0:T(8,128)(2,1)} %bitcast.7, bf16[560,2240]{1,0:T(8,128)(2,1)} %bitcast.8, bf16[560,2240]{1,0:T(8,128)(2,1)} %bitcast.9), custom_call_target="tpu_custom_call" | custom-call | tf_op jit(solution)/shard_map/pallas_call | solution.py:281
  37.2 1.9 %copy.9 = bf16[512,560]{0,1:T(8,128)(2,1)} copy(bf16[512,560]{0,1:T(8,128)(2,1)} %bitcast.13) | data formatting | bytes 1146880
  39.1 1.9 %copy.10 = bf16[512,560]{0,1:T(8,128)(2,1)} copy(bf16[512,560]{0,1:T(8,128)(2,1)} %bitcast.12) | data formatting | bytes 1146880

commit v3 on v2

--- a/solution.py
+++ b/solution.py
@@ -24,7 +24,7 @@
     att_ref, att_t_ref,
     tok, tan, wq, wk, wv, load_sem,
     kbuf, vbuf, ktbuf, vtbuf, qbuf, qtbuf,
-    state, r1, abuf, r2, bbuf, r3, erecv, esend, xsend, full,
+    state, r1, abuf, r2, bbuf, r3, erecv, esend, xsend, full, slant, ratios, inverses,
     s1, q1, s2, q2, s3, q3, s4, q4, s5, q5, s6, q6, s7, q7,
 ):
     ny, nz = n_space // 2, n_tm // 2
@@ -46,8 +46,8 @@
         load(0, tok_hbm, tok), load(1, wk_hbm, wk), load(2, wv_hbm, wv),
         load(3, tan_hbm, tan), load(4, wq_hbm, wq),
     ]
-    for one in loads:
-        one.start()
+    loads[0].start()
+    loads[1].start()
 
     barrier = pltpu.get_barrier_semaphore()
     partners = [{"space": core_mate}, {"tm": x_mate}, {"tm": z_next}, {"tm": z_prev}]
@@ -197,8 +197,11 @@
         )
     loads[0].wait()
     loads[1].wait()
+    loads[2].start()
+    loads[3].start()
     project(tok, wk, kbuf)
     loads[2].wait()
+    loads[4].start()
     project(tok, wv, vbuf)
     over = ((1,), (1,))
     zero = jnp.zeros((), jnp.bfloat16)
@@ -231,33 +234,35 @@
     stage7(0)
     stage6(1)
     finish(0)
+
+    across = ((0,), (0,))
+
+    def maps_of(g, h):
+        seen = head(full.at[g], h)
+        high = seen.astype(jnp.bfloat16)
+        low = (seen - high.astype(jnp.float32)).astype(jnp.bfloat16)
+        return jnp.concatenate([high, low], axis=0)
+
+    def twice(a):
+        return jnp.concatenate([a, a], axis=0)
+
+    for h in range(HEADS):
+        queries = head(qbuf, h)
+        slope = jnp.where(queries > 0, head(qtbuf, h), zero)
+        maps = maps_of(0, h)
+        main = dot(maps, twice(jnp.maximum(queries, zero)), across)
+        slant[h] = dot(maps, twice(slope), across)
+        inverse = 1.0 / (main[HD : HD + 1] + EPSILON)
+        ratio = main[:HD] * inverse
+        inverses[h] = jnp.broadcast_to(inverse, inverses.shape[1:])
+        ratios[h] = ratio
+        att_ref[h * HD : (h + 1) * HD] = ratio.astype(att_ref.dtype)
     stage7(1)
     finish(1)
-
-    empty = jnp.zeros((HD, WIDE), jnp.float32)
     for h in range(HEADS):
-        queries = head(qbuf, h)
-        feature = jnp.maximum(queries, zero)
-        slope = jnp.where(queries > 0, head(qtbuf, h), zero)
-        sides = jnp.concatenate([feature, slope], axis=0)
-        seen, seen_t = head(full.at[0], h), head(full.at[1], h)
-        maps = jnp.concatenate(
-            [
-                jnp.concatenate([seen, seen_t], axis=1),
-                jnp.concatenate([empty, seen], axis=1),
-            ],
-            axis=0,
-        )
-        high = maps.astype(jnp.bfloat16)
-        low = (maps - high.astype(jnp.float32)).astype(jnp.bfloat16)
-        across = ((0,), (0,))
-        both = dot(high, sides, across) + dot(low, sides, across)
-        main, slant = both[:WIDE], both[WIDE:]
-        inverse = 1.0 / (main[HD : HD + 1] + EPSILON)
-        denom_t = slant[HD : HD + 1]
-        attended = main[:HD] * inverse
-        tangent = (slant[:HD] - attended * denom_t) * inverse
-        att_ref[h * HD : (h + 1) * HD] = attended.astype(att_ref.dtype)
+        feature = jnp.maximum(head(qbuf, h), zero)
+        change = slant[h] + dot(maps_of(1, h), twice(feature), across)
+        tangent = (change[:HD] - ratios[h] * change[HD : HD + 1]) * inverses[h, :1]
         att_t_ref[h * HD : (h + 1) * HD] = tangent.astype(att_t_ref.dtype)
     for g in range(2):
         drain(g)
@@ -280,8 +285,8 @@
             sems += [dma(shape), dma(shape)]
         outs = pl.pallas_call(
             functools.partial(kernel, n_tm, n_space, rows),
-            out_shape=[jax.ShapeDtypeStruct((out, count), bf16)] * 2,
-            in_specs=[pl.BlockSpec(memory_space=pl.ANY)] * 5,
+            out_shape=[pltpu.VMEM((out, count), bf16)] * 2,
+            in_specs=[pl.BlockSpec(memory_space=pltpu.HBM)] * 5,
             out_specs=[pl.BlockSpec(memory_space=pltpu.VMEM)] * 2,
             scratch_shapes=[
                 pltpu.VMEM((width, count), bf16),
@@ -303,10 +308,13 @@
                 pltpu.VMEM((2, eighth, WIDE), f32),
                 pltpu.VMEM((2, eighth, WIDE), f32),
                 pltpu.VMEM((2, rows, WIDE), f32),
+                pltpu.VMEM((HEADS, WIDE, count), f32),
+                pltpu.VMEM((HEADS, HD, count), f32),
+                pltpu.VMEM((HEADS, 8, count), f32),
             ]
             + sems,
             compiler_params=pltpu.CompilerParams(
-                collective_id=0, has_side_effects=True, vmem_limit_bytes=60 * 1024 * 1024
+                collective_id=0, has_side_effects=True, vmem_limit_bytes=57 * 1024 * 1024
             ),
         )(tokens.T, tangents.T, w_query.T, w_key.T, w_value.T)
         return outs[0].T, outs[1].T

time: 41.2 us -> 37.7 us (0.915)
  local copies, waits for them, and re-layouts: 3.81 us -> 1.62 us
  Pallas kernels: 36.6 us -> 35.3 us
    unnamed x2, local copies, waits for them, and re-layouts: 3.81 us -> 1.62 us
    pallas_call x1, Pallas kernels: 36.6 us -> 35.3 us  [step(): pl.pallas_call(functools.partial(kernel, n_tm, n_space, rows), out_shape=...]
where the time goes in v3:
time: 37.7 us; the launch traced here: 37.5 us
  Pallas kernels  35.3 us (94%)
  local copies, waits for them, and re-layouts  1.62 us (4%)
  between operations  0.64 us (2%)
    pallas_call x1, Pallas kernels, step(): pl.pallas_call(functools.partial(kernel, n_tm, n_space, rows), out_shape=...  35.3 us
    unnamed x2, local copies, waits for them, and re-layouts  1.62 us

profile of v3, /device:TPU:27, one launch (start us, length us, event | category | flops | bytes accessed | tf_op | source)
XLA Modules:
  0.0 37.5 jit_solution(11809105018504022708)
XLA Ops:
  0.6 35.3 %shard_map.68 = (bf16[560,512]{1,0:T(8,128)(2,1)S(1)}, bf16[560,512]{1,0:T(8,128)(2,1)S(1)}) custom-call(bf16[2240,512]{1,0:T(8,128)(2,1)} %bitcast.12, bf16[2240,512]{1,0:T(8,128)(2,1)} %bitcast.13, bf16[560,2240]{1,0:T(8,128)(2,1)} %bitcast.9, bf16[560,2240]{1,0:T(8,128)(2,1)} %bitcast.10, bf16[560,2240]{1,0:T(8,128)(2,1)} %bitcast.11), custom_call_target="tpu_custom_call" | custom-call | tf_op jit(solution)/shard_map/pallas_call | solution.py:286
  35.9 0.8 %copy.9 = bf16[512,560]{0,1:T(8,128)(2,1)} copy(bf16[512,560]{0,1:T(8,128)(2,1)S(1)} %bitcast.8) | data formatting | bytes 1146880
  36.7 0.8 %copy.10 = bf16[512,560]{0,1:T(8,128)(2,1)} copy(bf16[512,560]{0,1:T(8,128)(2,1)S(1)} %bitcast.7) | data formatting | bytes 1146880

commit v4 on v3

--- a/solution.py
+++ b/solution.py
@@ -85,13 +85,21 @@
             s3.at[g], q3.at[g], {"tm": x_mate},
         )
 
-    def copy4(g):
-        return send(esend.at[g], erecv.at[g], s4.at[g], q4.at[g], {"tm": z_next})
-
-    def copy5(g):
-        return send(
-            xsend.at[g], full.at[g, rows_at(quarter_mine + x * eighth, eighth)],
-            s5.at[g], q5.at[g], {"tm": x_mate},
+    cut = (eighth // 8 + 1) // 2 * 8
+    pieces = [(0, cut), (cut, eighth - cut)]
+
+    def copy4(g, j):
+        part = pl.ds(*pieces[j])
+        return send(
+            esend.at[g, part], erecv.at[g, part], s4.at[g, j], q4.at[g, j], {"tm": z_next}
+        )
+
+    def copy5(g, j):
+        start, size = pieces[j]
+        return send(
+            xsend.at[g, pl.ds(start, size)],
+            full.at[g, rows_at(quarter_mine + x * eighth + start, size)],
+            s5.at[g, j], q5.at[g, j], {"tm": x_mate},
         )
 
     def copy6(g, k):
@@ -121,34 +129,40 @@
 
     def stage4(g):
         copy3(g).wait_recv()
-        own = bbuf[g, rows_at(x * eighth, eighth)]
+        for j, (start, size) in enumerate(pieces):
+            piece(g, j, start, size)
+
+    def piece(g, j, start, size):
+        part = pl.ds(start, size)
+        own = bbuf[g, rows_at(x * eighth + start, size)]
 
         @pl.when(z == 0)
         def _():
-            erecv[g] = jnp.zeros((eighth, WIDE), jnp.float32)
+            erecv[g, part] = jnp.zeros((size, WIDE), jnp.float32)
 
         @pl.when(z > 0)
         def _():
-            copy4(g).wait_recv()
-
-        before, other = erecv[g], r3[g]
+            copy4(g, j).wait_recv()
+
+        before, other = erecv[g, part], r3[g, part]
         first = before + other
         pair = first + own
 
         @pl.when(z < nz - 1)
         def _():
-            esend[g] = pair
-            copy4(g).start()
+            esend[g, part] = pair
+            copy4(g, j).start()
 
         mine_first = x == 0
-        xsend[g] = jnp.where(mine_first, pair, first)
-        copy5(g).start()
-        full[g, rows_at(quarter_mine + x * eighth, eighth)] = jnp.where(
+        xsend[g, part] = jnp.where(mine_first, pair, first)
+        copy5(g, j).start()
+        full[g, rows_at(quarter_mine + x * eighth + start, size)] = jnp.where(
             mine_first, before + own, pair
         )
 
     def stage6(g):
-        copy5(g).wait_recv()
+        for j in range(2):
+            copy5(g, j).wait_recv()
         for k in range(1, ny):
             copy6(g, k).start()
         copy7(g, 0).start()
@@ -171,9 +185,11 @@
 
         @pl.when(z < nz - 1)
         def _():
-            copy4(g).wait_send()
-
-        copy5(g).wait_send()
+            for j in range(2):
+                copy4(g, j).wait_send()
+
+        for j in range(2):
+            copy5(g, j).wait_send()
         for k in range(ny):
             copy7(g, k).wait_send()
 
@@ -281,7 +297,7 @@
         quarter, eighth = rows // n_space, rows // (2 * n_space)
         dma = pltpu.SemaphoreType.DMA
         sems = []
-        for shape in ((2,), (2, ny - 1), (2,), (2,), (2,), (2, ny - 1), (2, ny)):
+        for shape in ((2,), (2, ny - 1), (2,), (2, 2), (2, 2), (2, ny - 1), (2, ny)):
             sems += [dma(shape), dma(shape)]
         outs = pl.pallas_call(
             functools.partial(kernel, n_tm, n_space, rows),

time: 37.7 us -> 37.6 us (level)
  no operation moved by 1% of the time
where the time goes in v4:
time: 37.6 us; the launch traced here: 37.4 us
  Pallas kernels  35.2 us (94%)
  local copies, waits for them, and re-layouts  1.62 us (4%)
  between operations  0.64 us (2%)
    pallas_call x1, Pallas kernels, step(): pl.pallas_call(functools.partial(kernel, n_tm, n_space, rows), out_shape=...  35.2 us
    unnamed x2, local copies, waits for them, and re-layouts  1.62 us

profile of v4, /device:TPU:27, one launch (start us, length us, event | category | flops | bytes accessed | tf_op | source)
XLA Modules:
  0.0 37.4 jit_solution(5241236072563498930)
XLA Ops:
  0.6 35.2 %shard_map.68 = (bf16[560,512]{1,0:T(8,128)(2,1)S(1)}, bf16[560,512]{1,0:T(8,128)(2,1)S(1)}) custom-call(bf16[2240,512]{1,0:T(8,128)(2,1)} %bitcast.12, bf16[2240,512]{1,0:T(8,128)(2,1)} %bitcast.13, bf16[560,2240]{1,0:T(8,128)(2,1)} %bitcast.9, bf16[560,2240]{1,0:T(8,128)(2,1)} %bitcast.10, bf16[560,2240]{1,0:T(8,128)(2,1)} %bitcast.11), custom_call_target="tpu_custom_call" | custom-call | tf_op jit(solution)/shard_map/pallas_call | solution.py:302
  35.8 0.8 %copy.9 = bf16[512,560]{0,1:T(8,128)(2,1)} copy(bf16[512,560]{0,1:T(8,128)(2,1)S(1)} %bitcast.8) | data formatting | bytes 1146880
  36.6 0.8 %copy.10 = bf16[512,560]{0,1:T(8,128)(2,1)} copy(bf16[512,560]{0,1:T(8,128)(2,1)S(1)} %bitcast.7) | data formatting | bytes 1146880

commit v5 on v4

--- a/solution.py
+++ b/solution.py
@@ -242,9 +242,9 @@
     loads[4].wait()
     project(tok, wq, qbuf)
     stage2(1)
-    stage4(0)
     project(tan, wq, qtbuf)
     stage3(1)
+    stage4(0)
     stage4(1)
     stage6(0)
     stage7(0)

time: 37.6 us -> 37.2 us (0.989); the launches traced: 37.4 us -> 36.5 us
  Pallas kernels: 35.2 us -> 34.3 us
    pallas_call x1, Pallas kernels: 35.2 us -> 34.3 us  [step(): pl.pallas_call(functools.partial(kernel, n_tm, n_space, rows), out_shape=...]
where the time goes in v5:
time: 37.2 us; the launch traced here: 36.5 us
  Pallas kernels  34.3 us (92%)
  local copies, waits for them, and re-layouts  1.62 us (4%)
  between operations  0.64 us (2%)
    pallas_call x1, Pallas kernels, step(): pl.pallas_call(functools.partial(kernel, n_tm, n_space, rows), out_shape=...  34.3 us
    unnamed x2, local copies, waits for them, and re-layouts  1.62 us

profile of v5, /device:TPU:27, one launch (start us, length us, event | category | flops | bytes accessed | tf_op | source)
XLA Modules:
  0.0 36.5 jit_solution(13934577723755118457)
XLA Ops:
  0.6 34.3 %shard_map.68 = (bf16[560,512]{1,0:T(8,128)(2,1)S(1)}, bf16[560,512]{1,0:T(8,128)(2,1)S(1)}) custom-call(bf16[2240,512]{1,0:T(8,128)(2,1)} %bitcast.12, bf16[2240,512]{1,0:T(8,128)(2,1)} %bitcast.13, bf16[560,2240]{1,0:T(8,128)(2,1)} %bitcast.9, bf16[560,2240]{1,0:T(8,128)(2,1)} %bitcast.10, bf16[560,2240]{1,0:T(8,128)(2,1)} %bitcast.11), custom_call_target="tpu_custom_call" | custom-call | tf_op jit(solution)/shard_map/pallas_call | solution.py:302
  34.9 0.8 %copy.9 = bf16[512,560]{0,1:T(8,128)(2,1)} copy(bf16[512,560]{0,1:T(8,128)(2,1)S(1)} %bitcast.8) | data formatting | bytes 1146880
  35.7 0.8 %copy.10 = bf16[512,560]{0,1:T(8,128)(2,1)} copy(bf16[512,560]{0,1:T(8,128)(2,1)S(1)} %bitcast.7) | data formatting | bytes 1146880
